TPU v7x, 512 devices: a whole 4x8x8 slice. The times are simulated.
512 devices in a mesh: rows: 16 (over x, y_lo, core), pairs: 32 (over y_hi, z).
Axes of the slice: x: 4, y: 8 (y_hi: 4, y_lo: 2; y = y_hi * 2 + y_lo), z: 8, core: 2. Of those that a mesh axis runs over, the one named last changes fastest.
Arguments:
- snapshots: float32 [32768, 8192], P('rows', 'pairs'), may hold values from -1600 to 1600, as said below
Outputs:
- rotated: float32 [32768, 8192], P('rows', 'pairs')
Inputs may be any that keep to these rules, and one draw needn't show every extreme that they name: `snapshots`: finite real values.
All inputs are finite; a program needn't handle non-finite values.
Results may differ from a plain program's by a relative error of at most 0.00011.
Values sent between devices are 32-bit elements; how exact they have to be, the bound alone decides.
A program may use at most 64 MiB of HBM per device.

v0:
```python
import jax
import jax.numpy as jnp
from jax import lax
from jax.sharding import PartitionSpec as P


def from_behind(value, axis, steps):
    count = lax.axis_size(axis)
    leading, last = (max(0, -steps), min(count, count - steps))
    return lax.ppermute(value, axis, [(source, source + steps) for source in range(leading, last)])


def gram_of(left, right):
    return lax.dot_general(left, right, (((0,), (0,)), ((), ())), precision=lax.Precision.HIGHEST)


def finish(pair, gram, total):
    scaled = gram / total
    identity = jnp.eye(gram.shape[0], dtype=pair.dtype)
    level = jnp.trace(scaled) / gram.shape[0]
    lower = jnp.linalg.cholesky(scaled + 0.1 * level * identity)
    inverse = lax.linalg.triangular_solve(lower, identity, left_side=True, lower=True)
    return jnp.dot(pair, inverse.T, precision=lax.Precision.HIGHEST)


def per_device(snapshots):
    local_rows = snapshots.shape[0]
    total = local_rows * lax.axis_size("rows")
    width = snapshots.shape[1] // 2
    count = lax.axis_size("pairs")
    index = lax.axis_index("pairs")
    first = index == 0
    last = index == count - 1
    pair = snapshots
    gram = lax.psum(gram_of(pair, pair), "rows")
    pair = finish(pair, gram, total)
    top = pair[:, :width]
    bottom = pair[:, width:]
    outgoing = jnp.where(first, bottom, top)
    arrived_top = from_behind(outgoing, "pairs", 1)
    arrived_bottom = from_behind(bottom, "pairs", -1)
    top_next = jnp.where(first, top, arrived_top)
    bottom_next = jnp.where(last, top, arrived_bottom)
    pair = jnp.concatenate([top_next, bottom_next], axis=1)
    gram = lax.psum(gram_of(pair, pair), "rows")
    pair = finish(pair, gram, total)
    return pair


def solution(mesh):
    return jax.shard_map(
        per_device,
        mesh=mesh,
        in_specs=(P("rows", "pairs"),),
        out_specs=P("rows", "pairs"),
        check_vma=False,
    )
```

profile of v0, /device:TPU:1, one launch (start us, length us, event | category | flops | bytes accessed | tf_op | source)
XLA Modules:
  0.0 497.8 jit_solution(18300253455600902669)
XLA Ops:
  6.5 1.6 copy-done
  8.1 4.2 fusion.30
  12.8 131.7 %all-reduce.4.cloned.1.call-done = f32[256,256]{0,1:T(8,128)} async-done(((f32[256,256]{0,1:T(8,128)}), f32[256,256]{0,1:T(8,128)}) %all-reduce.4.cloned.1.call-update) | async-done | bytes 262160 | tf_op jit(solution)/shard_map/psum | solution.py:35
  144.5 1.6 select_reduce_fusion.1
  148.9 11.7 %cholesky.130 = f32[128,128]{1,0:T(8,128)S(1)} custom-call(f32[128,128]{1,0:T(8,128)S(1)} %cholesky.194), custom_call_target="Cholesky" | custom-call | tf_op jit(solution)/shard_map/jit(cholesky)/cholesky | solution.py:21
  160.6 9.8 %custom-call.13 = f32[1,128,128]{1,2,0:T(8,128)S(1)} custom-call(f32[1,128,128]{2,1,0:T(8,128)S(1)} %get-tuple-element.54), custom_call_target="InvertDiagBlocksLowerTriangular" | custom-call | tf_op jit(solution)/shard_map/jit(cholesky)/cholesky | solution.py:21
  170.9 11.7 %cholesky.147 = f32[128,128]{1,0:T(8,128)S(1)} custom-call(f32[128,128]{1,0:T(8,128)S(1)} %convolution_subtract_fusion.3), custom_call_target="Cholesky" | custom-call | tf_op jit(solution)/shard_map/jit(cholesky)/cholesky | solution.py:21
  184.9 16.2 %while.4 = (s32[]{:T(128)}, f32[256,256]{1,0:T(8,128)S(1)}, s32[2,2]{1,0:T(2,128)S(1)}, f32[2,128,128]{2,1,0:T(8,128)S(1)}, s32[]{:T(128)}) while((s32[]{:T(128)}, f32[256,256]{1,0:T(8,128)S(1)}, s32[2,2]{1,0:T(2,128)S(1)}, f32[2,128,128]{2,1,0:T(8,128)S(1)}, s32[]{:T(128)}) %tuple.45), condition=%wide.while_cond, body=%wide.while_body.sunk | while | flops 2 | bytes 131181 | solution.py:22
  197.6 1.4 bitcast_dynamic-update-slice_fusion.4
  199.6 1.4 bitcast_dynamic-update-slice_fusion.4
  201.1 19.7 %custom-call.14 = f32[2,128,128]{1,2,0:T(8,128)S(1)} custom-call(f32[2,128,128]{2,1,0:T(8,128)S(1)} %get-tuple-element.21), custom_call_target="InvertDiagBlocksLowerTriangular" | custom-call | tf_op jit(solution)/shard_map/triangular_solve/custom-call.0 | solution.py:22
  221.8 1.9 convolution_bitcast_fusion
  223.8 1.4 slice_select_fusion.2
  225.4 4.3 collective-permute-start
  231.0 19.8 %collective-permute-done = f32[2048,128]{0,1:T(8,128)} collective-permute-done((f32[2048,128]{0,1:T(8,128)}, f32[2048,128]{0,1:T(8,128)}, u32[]{:S(2)}, u32[]{:S(2)}) %collective-permute-start) | collective-permute-done | bytes 1048608 | tf_op jit(solution)/shard_map/ppermute | solution.py:10
  250.8 4.6 collective-permute-done.1
  255.4 1.7 slice_select_fusion.1
  258.2 2.6 fusion.1
  260.8 145.7 %all-reduce.6.cloned.1.call-done = f32[256,256]{0,1:T(8,128)} async-done(((f32[256,256]{0,1:T(8,128)}), f32[256,256]{0,1:T(8,128)}) %all-reduce.6.cloned.1.call-update) | async-done | bytes 262160 | tf_op jit(solution)/shard_map/psum | solution.py:45
  406.4 1.6 select_reduce_fusion
  408.7 1.7 select_add_fusion
  410.4 1.8 copy.5
  414.0 11.7 %cholesky.164 = f32[128,128]{1,0:T(8,128)S(1)} custom-call(f32[128,128]{1,0:T(8,128)S(1)} %cholesky.197), custom_call_target="Cholesky" | custom-call | tf_op jit(solution)/shard_map/jit(cholesky)/cholesky | solution.py:21
  426.4 9.8 %custom-call.15 = f32[1,128,128]{1,2,0:T(8,128)S(1)} custom-call(f32[1,128,128]{2,1,0:T(8,128)S(1)} %get-tuple-element.50), custom_call_target="InvertDiagBlocksLowerTriangular" | custom-call | tf_op jit(solution)/shard_map/jit(cholesky)/cholesky | solution.py:21
  436.3 1.7 constant_dynamic-update-slice_fusion.1
  439.0 11.9 %cholesky.181 = f32[128,128]{1,0:T(8,128)S(1)} custom-call(f32[128,128]{1,0:T(8,128)S(1)} %convolution_subtract_fusion.2), custom_call_target="Cholesky" | custom-call | tf_op jit(solution)/shard_map/jit(cholesky)/cholesky | solution.py:21
  454.2 1.7 select_select_fusion
  455.9 5.8 %while.5 = (s32[]{:T(128)}, f32[256,256]{1,0:T(8,128)}, s32[2,2]{1,0:T(2,128)S(1)}, f32[2,128,128]{2,1,0:T(8,128)S(1)}, s32[]{:T(128)}) while((s32[]{:T(128)}, f32[256,256]{1,0:T(8,128)}, s32[2,2]{1,0:T(2,128)S(1)}, f32[2,128,128]{2,1,0:T(8,128)S(1)}, s32[]{:T(128)}) %tuple.55), condition=%wide.while_cond.clone, body=%wide.while_body.clone.sunk | while | flops 2 | bytes 131181 | solution.py:22
  456.5 2.3 bitcast_dynamic-update-slice_fusion.5
  459.5 2.2 bitcast_dynamic-update-slice_fusion.5
  462.3 20.5 %custom-call.16 = f32[2,128,128]{1,2,0:T(8,128)S(1)} custom-call(f32[2,128,128]{2,1,0:T(8,128)} %copy-done.4), custom_call_target="InvertDiagBlocksLowerTriangular" | custom-call | tf_op jit(solution)/shard_map/triangular_solve/custom-call.0 | solution.py:22
  484.7 6.0 %fusion = f32[2048,256]{1,0:T(8,128)} fusion(f32[2048,128]{0,1:T(8,128)} %copy-done.2, f32[2048,128]{0,1:T(8,128)S(1)} %get-tuple-element.43, f32[128,256]{1,0:T(8,128)S(1)} %fusion.16, f32[128,256]{1,0:T(8,128)S(1)} %fusion.11), kind=kOutput, calls=%fused_computation.6 | convolution fusion | flops 1611202560 | bytes 4456448 | tf_op jit(solution)/shard_map/dot_general | solution.py:23
  (52 shorter events, 18.3 us)
Async XLA Ops:
  6.5 1.6 copy-start
  6.5 137.9 %all-reduce.4.cloned.1.call-start = ((), (), s32[]{:S(2)}) async-start(), calls=%async_computation | async-start | bytes 524288 | tf_op jit(solution)/shard_map/psum | solution.py:35
  12.3 394.1 %all-reduce.6.cloned.1.call-start = ((), (), s32[]{:S(2)}) async-start(), calls=%async_computation.1 | async-start | bytes 524288 | tf_op jit(solution)/shard_map/psum | solution.py:45
  223.8 1.7 copy-start.1
  225.4 25.4 %collective-permute-start = (f32[2048,128]{0,1:T(8,128)}, f32[2048,128]{0,1:T(8,128)}, u32[]{:S(2)}, u32[]{:S(2)}) collective-permute-start(f32[2048,128]{0,1:T(8,128)} %get-tuple-element.45), channel_id=1, source_target_pairs={{0,1},{1,2},{2,3},{3,4},{4,5},{5,6},{6,7},{7,8},{8,9},{9,10},{10,1... | collective-permute-start | bytes 3145736 | tf_op jit(solution)/shard_map/ppermute | solution.py:10
  229.7 25.7 %collective-permute-start.1 = (f32[2048,128]{0,1:T(8,128)S(1)}, f32[2048,128]{0,1:T(8,128)}, u32[]{:S(2)}, u32[]{:S(2)}) collective-permute-start(f32[2048,128]{0,1:T(8,128)S(1)} %get-tuple-element.46), channel_id=1, source_target_pairs={{1,0},{2,1},{3,2},{4,3},{5,4},{6,5},{7,6},{8,7},{9,8},{10,9},{11,1... | collective-permute-start | bytes 3145736 | tf_op jit(solution)/shard_map/ppermute | solution.py:10
  257.2 1.0 copy-start.2
  413.2 0.7 copy-start.3
  461.7 0.6 copy-start.4
Sparse Core Ops, SparseCore 0:
  12.4 132.0 all-reduce.3
  260.9 145.5 all-reduce.5
where the time goes:
time: 502 us; the launch traced here: 498 us
  waiting for transfers between devices  302 us (60%)
  other arithmetic  122 us (24%)
  matrix products  20.8 us (4%)
  between operations  17.8 us (4%)
  local copies, waits for them, and re-layouts  16.8 us (3%)
  loops' own time  12.2 us (2%)
  starting transfers between devices  6 us (1%)
    psum x2, waiting for transfers between devices, per_device(): gram = lax.psum(gram_of(pair, pair), 'rows')  277 us
    another operation x13, other arithmetic, finish(): lower = jnp.linalg.cholesky(scaled + 0.1 * level * identity)  69.5 us
    another operation x5, other arithmetic, finish(): lax.linalg.triangular_solve(lower, identity, left_side=True, lower=True)  41.9 us
    ppermute x2, waiting for transfers between devices, from_behind(): lax.ppermute(value, axis, [(source, source + steps) for source in range(l...  24.4 us
    another operation x2, loops' own time, finish(): lax.linalg.triangular_solve(lower, identity, left_side=True, lower=True)  12.2 us
  transfers between devices with their start and end apart: 4, of which 4 were waited for; matrix products, arithmetic and copies ran while one was open for 0% of the time, Pallas kernels for 0%

commit v1 on v0

--- a/solution.py
+++ b/solution.py
@@ -32,7 +32,7 @@
     first = index == 0
     last = index == count - 1
     pair = snapshots
-    gram = lax.psum(gram_of(pair, pair), "rows")
+    gram = jnp.sum(lax.all_gather(gram_of(pair, pair), "rows"), axis=0)
     pair = finish(pair, gram, total)
     top = pair[:, :width]
     bottom = pair[:, width:]

time: 502 us -> 422 us (0.84)
  waiting for transfers between devices: 302 us -> 222 us
    psum x2 -> x1, waiting for transfers between devices: 277 us -> 149 us  [per_device(): gram = lax.psum(gram_of(pair, pair), 'rows')]
    all_gather x0 -> x1, waiting for transfers between devices: none -> 48.2 us  [per_device(): gram = jnp.sum(lax.all_gather(gram_of(pair, pair), 'rows'), axis=0)]
where the time goes in v1:
time: 422 us; the launch traced here: 418 us
  waiting for transfers between devices  222 us (53%)
  other arithmetic  122 us (29%)
  matrix products  20.8 us (5%)
  between operations  17.8 us (4%)
  local copies, waits for them, and re-layouts  17 us (4%)
  loops' own time  12.2 us (3%)
  starting transfers between devices  6 us (1%)
    psum x1, waiting for transfers between devices, per_device(): gram = lax.psum(gram_of(pair, pair), 'rows')  149 us
    another operation x13, other arithmetic, finish(): lower = jnp.linalg.cholesky(scaled + 0.1 * level * identity)  69.5 us
    all_gather x1, waiting for transfers between devices, per_device(): gram = jnp.sum(lax.all_gather(gram_of(pair, pair), 'rows'), axis=0)  48.2 us
    another operation x5, other arithmetic, finish(): lax.linalg.triangular_solve(lower, identity, left_side=True, lower=True)  41.9 us
    ppermute x2, waiting for transfers between devices, from_behind(): lax.ppermute(value, axis, [(source, source + steps) for source in range(l...  24.9 us
    another operation x2, loops' own time, finish(): lax.linalg.triangular_solve(lower, identity, left_side=True, lower=True)  12.2 us
    another operation x15, local copies, waits for them, and re-layouts, finish(): lax.linalg.triangular_solve(lower, identity, left_side=True, lower=True)  9.92 us
  transfers between devices with their start and end apart: 4, of which 4 were waited for; matrix products, arithmetic and copies ran while one was open for 0% of the time, Pallas kernels for 0%

profile of v1, /device:TPU:1, one launch (start us, length us, event | category | flops | bytes accessed | tf_op | source)
XLA Modules:
  0.0 417.6 jit_solution(9291367935673095638)
XLA Ops:
  6.5 1.6 copy-done
  8.1 4.2 %fusion.30 = f32[256,256]{1,0:T(8,128)} fusion(f32[2048,256]{1,0:T(8,128)S(1)} %copy-done), kind=kOutput, calls=%fused_computation.74 | convolution fusion | flops 1610612736 | bytes 2359296 | tf_op jit(solution)/shard_map/dot_general | solution.py:14
  12.8 48.2 %all-gather.3.cloned.1.call-done = f32[4096,256]{1,0:T(8,128)} async-done(((f32[256,256]{1,0:T(8,128)}), f32[4096,256]{1,0:T(8,128)}) %all-gather.3.cloned.1.call-update) | async-done | bytes 4194320 | tf_op jit(solution)/shard_map/all_gather | solution.py:35
  61.1 2.5 reduce_sum.25
  65.2 11.7 %cholesky.130 = f32[128,128]{1,0:T(8,128)S(1)} custom-call(f32[128,128]{1,0:T(8,128)S(1)} %cholesky.194), custom_call_target="Cholesky" | custom-call | tf_op jit(solution)/shard_map/jit(cholesky)/cholesky | solution.py:21
  77.0 9.8 %custom-call.13 = f32[1,128,128]{1,2,0:T(8,128)S(1)} custom-call(f32[1,128,128]{2,1,0:T(8,128)S(1)} %get-tuple-element.54), custom_call_target="InvertDiagBlocksLowerTriangular" | custom-call | tf_op jit(solution)/shard_map/jit(cholesky)/cholesky | solution.py:21
  87.3 11.7 %cholesky.147 = f32[128,128]{1,0:T(8,128)S(1)} custom-call(f32[128,128]{1,0:T(8,128)S(1)} %convolution_subtract_fusion.3), custom_call_target="Cholesky" | custom-call | tf_op jit(solution)/shard_map/jit(cholesky)/cholesky | solution.py:21
  101.2 16.2 %while.4 = (s32[]{:T(128)}, f32[256,256]{1,0:T(8,128)S(1)}, s32[2,2]{1,0:T(2,128)S(1)}, f32[2,128,128]{2,1,0:T(8,128)S(1)}, s32[]{:T(128)}) while((s32[]{:T(128)}, f32[256,256]{1,0:T(8,128)S(1)}, s32[2,2]{1,0:T(2,128)S(1)}, f32[2,128,128]{2,1,0:T(8,128)S(1)}, s32[]{:T(128)}) %tuple.45), condition=%wide.while_cond, body=%wide.while_body.sunk | while | flops 2 | bytes 131181 | solution.py:22
  113.9 1.4 bitcast_dynamic-update-slice_fusion.4
  116.0 1.4 bitcast_dynamic-update-slice_fusion.4
  117.4 19.7 %custom-call.14 = f32[2,128,128]{1,2,0:T(8,128)S(1)} custom-call(f32[2,128,128]{2,1,0:T(8,128)S(1)} %get-tuple-element.21), custom_call_target="InvertDiagBlocksLowerTriangular" | custom-call | tf_op jit(solution)/shard_map/triangular_solve/custom-call.0 | solution.py:22
  138.1 1.9 convolution_bitcast_fusion
  140.1 1.4 slice_select_fusion.2
  141.8 4.3 %collective-permute-start = (f32[2048,128]{0,1:T(8,128)}, f32[2048,128]{0,1:T(8,128)}, u32[]{:S(2)}, u32[]{:S(2)}) collective-permute-start(f32[2048,128]{0,1:T(8,128)} %get-tuple-element.45), channel_id=1, source_target_pairs={{0,1},{1,2},{2,3},{3,4},{4,5},{5,6},{6,7},{7,8},{8,9},{9,10},{10,1... | collective-permute-start | bytes 3145736 | tf_op jit(solution)/shard_map/ppermute | solution.py:10
  147.4 20.3 %collective-permute-done = f32[2048,128]{0,1:T(8,128)} collective-permute-done((f32[2048,128]{0,1:T(8,128)}, f32[2048,128]{0,1:T(8,128)}, u32[]{:S(2)}, u32[]{:S(2)}) %collective-permute-start) | collective-permute-done | bytes 1048608 | tf_op jit(solution)/shard_map/ppermute | solution.py:10
  167.6 4.6 %collective-permute-done.1 = f32[2048,128]{0,1:T(8,128)} collective-permute-done((f32[2048,128]{0,1:T(8,128)S(1)}, f32[2048,128]{0,1:T(8,128)}, u32[]{:S(2)}, u32[]{:S(2)}) %collective-permute-start.1) | collective-permute-done | bytes 1048608 | tf_op jit(solution)/shard_map/ppermute | solution.py:10
  172.2 1.7 slice_select_fusion.1
  174.9 2.6 fusion.1
  177.5 148.7 %all-reduce.3.cloned.1.call-done = f32[256,256]{0,1:T(8,128)} async-done(((f32[256,256]{0,1:T(8,128)}), f32[256,256]{0,1:T(8,128)}) %all-reduce.3.cloned.1.call-update) | async-done | bytes 262160 | tf_op jit(solution)/shard_map/psum | solution.py:45
  326.3 1.6 select_reduce_fusion
  328.5 1.7 select_add_fusion
  330.2 1.8 copy.8
  333.8 11.7 %cholesky.164 = f32[128,128]{1,0:T(8,128)S(1)} custom-call(f32[128,128]{1,0:T(8,128)S(1)} %cholesky.197), custom_call_target="Cholesky" | custom-call | tf_op jit(solution)/shard_map/jit(cholesky)/cholesky | solution.py:21
  346.3 9.8 %custom-call.15 = f32[1,128,128]{1,2,0:T(8,128)S(1)} custom-call(f32[1,128,128]{2,1,0:T(8,128)S(1)} %get-tuple-element.50), custom_call_target="InvertDiagBlocksLowerTriangular" | custom-call | tf_op jit(solution)/shard_map/jit(cholesky)/cholesky | solution.py:21
  356.1 1.7 constant_dynamic-update-slice_fusion.1
  358.9 11.9 %cholesky.181 = f32[128,128]{1,0:T(8,128)S(1)} custom-call(f32[128,128]{1,0:T(8,128)S(1)} %convolution_subtract_fusion.2), custom_call_target="Cholesky" | custom-call | tf_op jit(solution)/shard_map/jit(cholesky)/cholesky | solution.py:21
  374.0 1.7 select_select_fusion
  375.7 5.8 %while.5 = (s32[]{:T(128)}, f32[256,256]{1,0:T(8,128)}, s32[2,2]{1,0:T(2,128)S(1)}, f32[2,128,128]{2,1,0:T(8,128)S(1)}, s32[]{:T(128)}) while((s32[]{:T(128)}, f32[256,256]{1,0:T(8,128)}, s32[2,2]{1,0:T(2,128)S(1)}, f32[2,128,128]{2,1,0:T(8,128)S(1)}, s32[]{:T(128)}) %tuple.55), condition=%wide.while_cond.clone, body=%wide.while_body.clone.sunk | while | flops 2 | bytes 131181 | solution.py:22
  376.4 2.3 bitcast_dynamic-update-slice_fusion.5
  379.3 2.2 bitcast_dynamic-update-slice_fusion.5
  382.2 20.5 %custom-call.16 = f32[2,128,128]{1,2,0:T(8,128)S(1)} custom-call(f32[2,128,128]{2,1,0:T(8,128)} %copy-done.4), custom_call_target="InvertDiagBlocksLowerTriangular" | custom-call | tf_op jit(solution)/shard_map/triangular_solve/custom-call.0 | solution.py:22
  404.5 6.0 %fusion = f32[2048,256]{1,0:T(8,128)} fusion(f32[2048,128]{0,1:T(8,128)} %copy-done.2, f32[2048,128]{0,1:T(8,128)S(1)} %get-tuple-element.43, f32[128,256]{1,0:T(8,128)S(1)} %fusion.16, f32[128,256]{1,0:T(8,128)S(1)} %fusion.11), kind=kOutput, calls=%fused_computation.6 | convolution fusion | flops 1611202560 | bytes 4456448 | tf_op jit(solution)/shard_map/dot_general | solution.py:23
  (54 shorter events, 17.1 us)
Async XLA Ops:
  6.5 1.6 copy-start
  6.5 54.5 %all-gather.3.cloned.1.call-start = ((), (), s32[]{:S(2)}) async-start(), calls=%async_computation.1 | async-start | bytes 4456448 | tf_op jit(solution)/shard_map/all_gather | solution.py:35
  12.3 313.9 %all-reduce.3.cloned.1.call-start = ((), (), s32[]{:S(2)}) async-start(), calls=%async_computation | async-start | bytes 524288 | tf_op jit(solution)/shard_map/psum | solution.py:45
  140.1 1.7 copy-start.1
  141.8 25.8 %collective-permute-start = (f32[2048,128]{0,1:T(8,128)}, f32[2048,128]{0,1:T(8,128)}, u32[]{:S(2)}, u32[]{:S(2)}) collective-permute-start(f32[2048,128]{0,1:T(8,128)} %get-tuple-element.45), channel_id=1, source_target_pairs={{0,1},{1,2},{2,3},{3,4},{4,5},{5,6},{6,7},{7,8},{8,9},{9,10},{10,1... | collective-permute-start | bytes 3145736 | tf_op jit(solution)/shard_map/ppermute | solution.py:10
  146.1 26.2 %collective-permute-start.1 = (f32[2048,128]{0,1:T(8,128)S(1)}, f32[2048,128]{0,1:T(8,128)}, u32[]{:S(2)}, u32[]{:S(2)}) collective-permute-start(f32[2048,128]{0,1:T(8,128)S(1)} %get-tuple-element.46), channel_id=1, source_target_pairs={{1,0},{2,1},{3,2},{4,3},{5,4},{6,5},{7,6},{8,7},{9,8},{10,9},{11,1... | collective-permute-start | bytes 3145736 | tf_op jit(solution)/shard_map/ppermute | solution.py:10
  174.0 1.0 copy-start.2
  333.1 0.7 copy-start.3
  381.5 0.6 copy-start.4
Sparse Core Ops, SparseCore 0:
  12.5 48.5 all-gather.2
  177.7 148.5 all-reduce.2
